TPU v7x, 256 devices: a whole 4x4x8 slice. The times are simulated.
256 devices in a mesh: dp: 4 (over x), space: 16 (over z_lo, y), tm: 4 (over z_hi, core).
Axes of the slice: x: 4, y: 4, z: 8 (z_hi: 2, z_lo: 4; z = z_hi * 4 + z_lo), core: 2. Of those that a mesh axis runs over, the one named last changes fastest.
Arguments:
- inputs: bfloat16 [4, 32, 64, 4096], P('dp', 'tm', None, 'space'), may hold values from -6 to 6
- grad_out: bfloat16 [4, 32, 64, 4096], P('dp', 'tm', None, 'space'), may hold values from -6 to 6
- conv_w: bfloat16 [2, 128, 64], replicated, may hold values from -0.5 to 0.5
- conv_b: float32 [128], replicated, may hold values from -3 to 3
- mix_w: bfloat16 [3, 64, 64], replicated, may hold values from -0.4375 to 0.4375
- mix_b: float32 [64], replicated, may hold values from -3 to 3
- adj_tiles: bfloat16 [32, 8, 128, 128], P('space'), may hold values from -0.1875 to 0.1875
- tile_cols: int32 [32, 8], P('space'), may hold values from 0 to 9, as said below
- send_rows: int32 [16, 16, 64], P('space'), may hold values from 0 to 255
- counts: int32 [16, 16], P('space'), may hold values from 0 to 64, as said below
Outputs:
- outputs: bfloat16 [4, 32, 64, 4096], P('dp', 'tm', None, 'space')
- grad_inputs: bfloat16 [4, 32, 64, 4096], P('dp', 'tm', None, 'space')
- grad_conv_w: float32 [2, 128, 64], replicated
- grad_conv_b: float32 [128], replicated
- grad_mix_w: float32 [3, 64, 64], replicated
- grad_mix_b: float32 [64], replicated
Inputs may be any that keep to these rules, and one draw needn't show every extreme that they name: counts[s, s] = 0; counts[0, 1] = 64. `tile_cols`: column blocks below 2 are the part's own sensor blocks, 2 + i the i-th block of 128 received slots in order of source part and slot; in each row block the first 4 ids are below 2, the others are not.
All inputs are finite; a program needn't handle non-finite values.
Results may differ from a plain program's by a relative error of at most 0.0058.
Values may be sent and summed in bfloat16 or wider, within the bound.
A program may use at most 64 MiB of HBM per device.

v0:
```python
import math
import jax
import jax.numpy as jnp
from jax import lax
from jax.sharding import PartitionSpec as P

DILATION_SIZE = 2


def from_behind(value, axis, steps):
    count = lax.axis_size(axis)
    leading, last = (max(0, -steps), min(count, count - steps))
    return lax.ppermute(value, axis, [(source, source + steps) for source in range(leading, last)])


def slot_mask(counts, slot_count, dtype):
    slots = lax.broadcasted_iota(jnp.int32, (counts.shape[1], slot_count), 1)
    return (slots < counts[0][:, None]).astype(dtype)


def pack_rows(field, send_rows, live_slots):
    picked = field[:, :, send_rows[0]] * live_slots
    return picked.reshape(field.shape[0], field.shape[1], -1)


def tile_product(extended, adj_tiles, tile_cols):
    timestep_count, chan_count = (extended.shape[0], extended.shape[1])
    blocks = extended.reshape(timestep_count, chan_count, -1, adj_tiles.shape[2])
    picked = blocks[:, :, tile_cols]
    return jnp.einsum("tcrkj,rkij->tcri", picked, adj_tiles, preferred_element_type=jnp.float32)


def forward_start(field, send_rows, live_slots):
    packed = pack_rows(field, send_rows, live_slots)
    own_part = None
    return (packed, own_part)


def forward_finish(field, received, adj_tiles, tile_cols):
    total = tile_product(jnp.concatenate([field, received], 2), adj_tiles, tile_cols)
    return total.reshape(field.shape).astype(jnp.bfloat16)


def back_start(grad, adj_tiles, tile_cols, send_rows):
    timestep_count, chan_count, sensor_count = grad.shape
    tile_size = adj_tiles.shape[2]
    row_blocks = sensor_count // tile_size
    half_slots = tile_cols.shape[1] // 2
    halo_blocks = send_rows.shape[1] * send_rows.shape[2] // tile_size
    blocks = grad.reshape(timestep_count, chan_count, row_blocks, tile_size)
    remote_terms = jnp.einsum(
        "tcri,rkij->tcrkj", blocks, adj_tiles[:, half_slots:], preferred_element_type=jnp.float32
    )
    remote_sums = jnp.zeros((timestep_count, chan_count, halo_blocks, tile_size), jnp.float32)
    remote_sums = remote_sums.at[:, :, tile_cols[:, half_slots:] - row_blocks].add(remote_terms)
    return remote_sums.reshape(timestep_count, chan_count, -1).astype(jnp.bfloat16)


def back_finish(grad, returned, adj_tiles, tile_cols, send_rows, live_slots):
    timestep_count, chan_count, sensor_count = grad.shape
    tile_size = adj_tiles.shape[2]
    row_blocks = sensor_count // tile_size
    half_slots = tile_cols.shape[1] // 2
    blocks = grad.reshape(timestep_count, chan_count, row_blocks, tile_size)
    own_terms = jnp.einsum(
        "tcri,rkij->tcrkj", blocks, adj_tiles[:, :half_slots], preferred_element_type=jnp.float32
    )
    total = jnp.zeros((timestep_count, chan_count, row_blocks, tile_size), jnp.float32)
    total = total.at[:, :, tile_cols[:, :half_slots]].add(own_terms).reshape(grad.shape)
    returned = returned.reshape(
        timestep_count, chan_count, send_rows.shape[1], send_rows.shape[2]
    ).astype(jnp.float32)
    return total.at[:, :, send_rows[0]].add(returned * live_slots.astype(jnp.float32))


def mixing_grads(sample_grad, fields):
    grad_mix_w = jnp.stack(
        [
            jnp.einsum("ton,tcn->oc", sample_grad, item, preferred_element_type=jnp.float32)
            for item in fields
        ]
    )
    grad_mix_b = jnp.sum(sample_grad.astype(jnp.float32), axis=(0, 2))
    return (grad_mix_w, grad_mix_b)


def body(inputs, grad_out, conv_w, conv_b, mix_w, mix_b, adj_tiles, tile_cols, send_rows, counts):
    sample_input = inputs[0]
    sample_grad = grad_out[0]
    timestep_count, chan_count, sensor_count = sample_input.shape
    live_slots = slot_mask(counts, send_rows.shape[2], jnp.bfloat16)
    prior_border_slice = from_behind(sample_input[timestep_count - DILATION_SIZE :], "tm", 1)
    preceding_window = jnp.concatenate(
        [prior_border_slice, sample_input[: timestep_count - DILATION_SIZE]], 0
    )
    preact = jnp.einsum("oc,tcn->ton", conv_w[1], sample_input, preferred_element_type=jnp.float32)
    preact = preact + jnp.einsum(
        "oc,tcn->ton", conv_w[0], preceding_window, preferred_element_type=jnp.float32
    )
    preact = preact + conv_b[None, :, None]
    filtered = jnp.tanh(preact[:, :chan_count])
    gating = jax.nn.sigmoid(preact[:, chan_count:])
    hidden = (filtered * gating).astype(jnp.bfloat16)
    grad_float = sample_grad.astype(jnp.float32)
    packed_one, early_one = forward_start(hidden, send_rows, live_slots)
    received_one = lax.all_to_all(packed_one, "space", split_axis=2, concat_axis=2, tiled=True)
    hop_one = forward_finish(hidden, received_one, adj_tiles, tile_cols)
    packed_two, early_two = forward_start(hop_one, send_rows, live_slots)
    received_two = lax.all_to_all(packed_two, "space", split_axis=2, concat_axis=2, tiled=True)
    hop_two = forward_finish(hop_one, received_two, adj_tiles, tile_cols)
    fields = (hidden, hop_one, hop_two)
    grad_mix_w, grad_mix_b = mixing_grads(sample_grad, fields)
    back_two = jnp.einsum(
        "oc,ton->tcn", mix_w[2], sample_grad, preferred_element_type=jnp.float32
    ).astype(jnp.bfloat16)
    returned_two = lax.all_to_all(
        back_start(back_two, adj_tiles, tile_cols, send_rows),
        "space",
        split_axis=2,
        concat_axis=2,
        tiled=True,
    )
    back_one = jnp.einsum("oc,ton->tcn", mix_w[1], sample_grad, preferred_element_type=jnp.float32)
    back_one = (
        back_one + back_finish(back_two, returned_two, adj_tiles, tile_cols, send_rows, live_slots)
    ).astype(jnp.bfloat16)
    returned_one = lax.all_to_all(
        back_start(back_one, adj_tiles, tile_cols, send_rows),
        "space",
        split_axis=2,
        concat_axis=2,
        tiled=True,
    )
    back_hidden = jnp.einsum(
        "oc,ton->tcn", mix_w[0], sample_grad, preferred_element_type=jnp.float32
    )
    back_hidden = back_hidden + back_finish(
        back_one, returned_one, adj_tiles, tile_cols, send_rows, live_slots
    )
    mixed = sample_input.astype(jnp.float32) + mix_b[None, :, None]
    for index in range(3):
        mixed = mixed + jnp.einsum(
            "oc,tcn->ton", mix_w[index], fields[index], preferred_element_type=jnp.float32
        )
    outputs = mixed.astype(jnp.bfloat16)[None]
    grad_filter = back_hidden * (1.0 - filtered * filtered) * gating
    grad_gate = back_hidden * filtered * gating * (1.0 - gating)
    backward_preactivation = jnp.concatenate([grad_filter, grad_gate], 1).astype(jnp.bfloat16)
    next_border_slice = from_behind(backward_preactivation[:DILATION_SIZE], "tm", -1)
    following_window = jnp.concatenate(
        [backward_preactivation[DILATION_SIZE:], next_border_slice], 0
    )
    grad_inputs = grad_float + jnp.einsum(
        "oc,ton->tcn", conv_w[1], backward_preactivation, preferred_element_type=jnp.float32
    )
    grad_inputs = grad_inputs + jnp.einsum(
        "oc,ton->tcn", conv_w[0], following_window, preferred_element_type=jnp.float32
    )
    grad_inputs = grad_inputs.astype(jnp.bfloat16)[None]
    grad_conv_w = jnp.stack(
        [
            jnp.einsum(
                "ton,tcn->oc",
                backward_preactivation,
                preceding_window,
                preferred_element_type=jnp.float32,
            ),
            jnp.einsum(
                "ton,tcn->oc",
                backward_preactivation,
                sample_input,
                preferred_element_type=jnp.float32,
            ),
        ]
    )
    grad_conv_b = jnp.sum(backward_preactivation.astype(jnp.float32), axis=(0, 2))
    grad_conv_w, grad_conv_b, grad_mix_w, grad_mix_b = lax.psum(
        (grad_conv_w, grad_conv_b, grad_mix_w, grad_mix_b), ("dp", "space", "tm")
    )
    cell_count = (
        inputs.shape[0]
        * timestep_count
        * sensor_count
        * lax.axis_size("dp")
        * lax.axis_size("space")
        * lax.axis_size("tm")
    )
    scale = 1.0 / math.sqrt(cell_count)
    return (
        outputs,
        grad_inputs,
        grad_conv_w * scale,
        grad_conv_b * scale,
        grad_mix_w * scale,
        grad_mix_b * scale,
    )


def solution(mesh):
    in_specs = (
        P("dp", "tm", None, "space"),
        P("dp", "tm", None, "space"),
        P(),
        P(),
        P(),
        P(),
        P("space", None, None, None),
        P("space", None),
        P("space", None, None),
        P("space", None),
    )
    out_specs = (P("dp", "tm", None, "space"), P("dp", "tm", None, "space"), P(), P(), P(), P())
    return jax.shard_map(body, mesh=mesh, in_specs=in_specs, out_specs=out_specs, check_vma=False)
```

profile of v0, /device:TPU:1, one launch (start us, length us, event | category | flops | bytes accessed | tf_op | source)
XLA Modules:
  0.0 680.7 jit_solution(10881315894750508709)
XLA Ops:
  9.4 1.4 convolution_bitcast_fusion.2
  10.7 1.5 copy.81
  12.5 3.5 scatter_fusion.1
  17.3 2.3 reshape.258
  19.6 9.2 %all-to-all-start.2 = ((bf16[16,2,16384]{2,1,0:T(2,128)(2,1)}), bf16[16,2,16384]{2,1,0:T(2,128)(2,1)}, u32[]{:S(2)}, u32[]{:S(2)}) async-start(bf16[16,2,16384]{2,1,0:T(2,128)(2,1)} %reshape.258), calls=%async_computation.2 | async-start | bytes 2097152 | tf_op jit(solution)/shard_map/all_to_all | solution.py:116
  29.7 1.9 scatter_fusion
  32.5 18.7 %all-to-all-done.2 = bf16[16,2,16384]{2,1,0:T(2,128)(2,1)} async-done(((bf16[16,2,16384]{2,1,0:T(2,128)(2,1)}), bf16[16,2,16384]{2,1,0:T(2,128)(2,1)}, u32[]{:S(2)}, u32[]{:S(2)}) %all-to-all-start.2) | async-done | bytes 1048608 | tf_op jit(solution)/shard_map/all_to_all | solution.py:116
  51.2 3.8 reshape.259
  55.0 3.1 convert_multiply_fusion.1
  58.1 71.3 %scatter_fusion.2 = f32[8,64,256]{1,0,2:T(8,128)S(1)} fusion(f32[8,64,256]{1,0,2:T(8,128)S(1)} %copy.84, s32[1024]{0:T(1024)S(1)} %reshape.131, f32[1024,8,64]{2,1,0:T(8,128)} %bitcast.273), kind=kCustom, calls=%fused_computation.6 | custom fusion | flops 524288 | bytes 6295552 | tf_op jit(solution)/shard_map/scatter-add | solution.py:73
  130.8 1.5 copy.89
  132.5 3.5 scatter_fusion.4
  137.2 2.1 copy.124
  139.3 2.3 reshape.260
  141.6 7.7 %all-to-all-start.3 = ((bf16[16,2,16384]{2,1,0:T(2,128)(2,1)}), bf16[16,2,16384]{2,1,0:T(2,128)(2,1)}, u32[]{:S(2)}, u32[]{:S(2)}) async-start(bf16[16,2,16384]{2,1,0:T(2,128)(2,1)} %reshape.260), calls=%async_computation.3 | async-start | bytes 2097152 | tf_op jit(solution)/shard_map/all_to_all | solution.py:127
  149.3 8.2 %collective-permute-start = (bf16[2,64,256]{2,1,0:T(8,128)(2,1)S(1)}, bf16[2,64,256]{2,1,0:T(8,128)(2,1)S(1)}, u32[]{:S(2)}, u32[]{:S(2)}) collective-permute-start(bf16[2,64,256]{2,1,0:T(8,128)(2,1)S(1)} %slice_bitcast_fusion.1), channel_id=1, source_target_pairs={{0,1},{1,2},{2,3},{4,5},{5,6},{6,7},{8,9},{9,10},{10,11},{12,13},{... | collective-permute-start | bytes 196616 | tf_op jit(solution)/shard_map/ppermute | solution.py:13
  158.2 7.7 %collective-permute-done = bf16[2,64,256]{2,1,0:T(8,128)(2,1)S(1)} collective-permute-done((bf16[2,64,256]{2,1,0:T(8,128)(2,1)S(1)}, bf16[2,64,256]{2,1,0:T(8,128)(2,1)S(1)}, u32[]{:S(2)}, u32[]{:S(2)}) %collective-permute-start) | collective-permute-done | bytes 65568 | tf_op jit(solution)/shard_map/ppermute | solution.py:13
  167.9 1.9 scatter_fusion.3
  170.5 1.6 all-to-all-done.3
  172.2 3.8 reshape.261
  175.9 3.1 convert_multiply_fusion
  179.0 71.3 %scatter_fusion.5 = f32[8,64,256]{1,0,2:T(8,128)S(1)} fusion(f32[8,64,256]{1,0,2:T(8,128)S(1)} %copy.92, s32[1024]{0:T(1024)S(1)} %reshape.131, f32[1024,8,64]{2,1,0:T(8,128)} %bitcast.272), kind=kCustom, calls=%fused_computation.9 | custom fusion | flops 524288 | bytes 6295552 | tf_op jit(solution)/shard_map/scatter-add | solution.py:73
  252.6 7.6 %gather_fusion = bf16[1024,8,64]{2,1,0:T(8,128)(2,1)} fusion(bf16[8,64,256]{1,0,2:T(8,128)(2,1)S(1)} %copy.63, s32[1024]{0:T(1024)S(1)} %broadcast_clamp_fusion), kind=kCustom, calls=%fused_computation | custom fusion | bytes 2101248 | tf_op jit(solution)/shard_map/gather | solution.py:22
  260.1 4.9 fusion.76
  265.1 2.2 reshape.254
  267.3 7.9 %all-to-all-start = ((bf16[16,2,16384]{2,1,0:T(2,128)(2,1)}), bf16[16,2,16384]{2,1,0:T(2,128)(2,1)S(1)}, u32[]{:S(2)}, u32[]{:S(2)}) async-start(bf16[16,2,16384]{2,1,0:T(2,128)(2,1)} %reshape.254), calls=%async_computation | async-start | bytes 2097152 | tf_op jit(solution)/shard_map/all_to_all | solution.py:106
  276.1 21.2 %all-to-all-done = bf16[16,2,16384]{2,1,0:T(2,128)(2,1)S(1)} async-done(((bf16[16,2,16384]{2,1,0:T(2,128)(2,1)}), bf16[16,2,16384]{2,1,0:T(2,128)(2,1)S(1)}, u32[]{:S(2)}, u32[]{:S(2)}) %all-to-all-start) | async-done | bytes 1048608 | tf_op jit(solution)/shard_map/all_to_all | solution.py:106
  297.3 2.3 reshape.255
  299.7 3.4 pad_maximum_fusion
  303.1 3.4 copy.65
  306.5 2.3 gather_fusion.1
  309.9 3.3 gather_fusion.2
  313.2 4.8 fusion.77
  318.0 4.7 reshape.256
  322.7 7.9 %all-to-all-start.1 = ((bf16[16,2,16384]{2,1,0:T(2,128)(2,1)}), bf16[16,2,16384]{2,1,0:T(2,128)(2,1)S(1)}, u32[]{:S(2)}, u32[]{:S(2)}) async-start(bf16[16,2,16384]{2,1,0:T(2,128)(2,1)} %reshape.256), calls=%async_computation.1 | async-start | bytes 2097152 | tf_op jit(solution)/shard_map/all_to_all | solution.py:109
  332.3 1.7 fusion.7
  334.0 1.7 fusion.4
  336.4 4.1 collective-permute-start.1
  340.7 236.7 %all-reduce.3.cloned.1.call-done = f32[2,128,64]{1,2,0:T(8,128)} async-done(((f32[2,128,64]{1,2,0:T(8,128)}), f32[2,128,64]{1,2,0:T(8,128)}) %all-reduce.3.cloned.1.call-update) | async-done | bytes 65552 | tf_op jit(solution)/shard_map/psum | solution.py:177
  577.4 1.5 broadcast_multiply_fusion.1
  578.9 2.1 fusion.13
  581.2 1.7 fusion.3
  582.9 2.3 reshape.257
  585.3 3.4 pad_maximum_fusion.1
  588.7 3.4 copy.71
  592.1 2.3 gather_fusion.3
  595.4 1.6 fusion.14
  597.1 75.0 %all-reduce = (f32[128]{0:T(128)S(1)}, f32[3,64,64]{1,2,0:T(8,128)S(1)}, f32[64]{0:T(128)S(1)}) all-reduce(f32[128]{0:T(128)S(1)} %convert_reduce_fusion, f32[3,64,64]{1,2,0:T(8,128)S(1)} %pad_maximum_fusion.6, f32[64]{0:T(128)S(1)} %convert_reduce_fusion.1), channel_id=1, replica_groups=mesh['dp'=4,'space'=16,'tm'=4] {'dp','space','tm'}, use_global_device_ids=true, to_apply=%region_8.0 | all-reduce | flops 12480 | bytes 99840 | tf_op jit(solution)/shard_map/psum | solution.py:177
  (119 shorter events, 21.2 us)
Async XLA Ops:
  17.3 11.6 %copy-start.1 = (bf16[2,8,128,128]{3,2,1,0:T(8,128)(2,1)S(1)}, bf16[2,8,128,128]{3,2,1,0:T(8,128)(2,1)}, u32[]{:S(2)}) copy-start(bf16[2,8,128,128]{3,2,1,0:T(8,128)(2,1)} %param.16) | copy-start | bytes 1572868
  19.6 31.6 %all-to-all-start.2 = ((bf16[16,2,16384]{2,1,0:T(2,128)(2,1)}), bf16[16,2,16384]{2,1,0:T(2,128)(2,1)}, u32[]{:S(2)}, u32[]{:S(2)}) async-start(bf16[16,2,16384]{2,1,0:T(2,128)(2,1)} %reshape.258), calls=%async_computation.2 | async-start | bytes 2097152 | tf_op jit(solution)/shard_map/all_to_all | solution.py:116
  29.7 1.9 copy-start
  29.7 1.9 copy-start.19
  31.6 0.7 copy-start.23
  31.6 0.8 copy-start.24
  129.3 1.0 copy-start.2
  139.3 10.0 %copy-start.12 = (bf16[1,8,64,256]{3,2,1,0:T(8,128)(2,1)S(1)}, bf16[1,8,64,256]{3,2,1,0:T(8,128)(2,1)}, u32[]{:S(2)}) copy-start(bf16[1,8,64,256]{3,2,1,0:T(8,128)(2,1)} %param.10) | copy-start | bytes 786436
  141.6 16.3 %copy-start.21 = (bf16[2,128,64]{1,2,0:T(8,128)(2,1)S(1)}, bf16[2,128,64]{1,2,0:T(8,128)(2,1)}, u32[]{:S(2)}) copy-start(bf16[2,128,64]{1,2,0:T(8,128)(2,1)} %param.12) | copy-start | bytes 98308
  141.6 24.3 %copy-start.26 = (f32[128]{0:T(128)S(1)}, f32[128]{0:T(128)}, u32[]{:S(2)}) copy-start(f32[128]{0:T(128)} %param.13) | copy-start | bytes 1540
  141.6 30.6 %all-to-all-start.3 = ((bf16[16,2,16384]{2,1,0:T(2,128)(2,1)}), bf16[16,2,16384]{2,1,0:T(2,128)(2,1)}, u32[]{:S(2)}, u32[]{:S(2)}) async-start(bf16[16,2,16384]{2,1,0:T(2,128)(2,1)} %reshape.260), calls=%async_computation.3 | async-start | bytes 2097152 | tf_op jit(solution)/shard_map/all_to_all | solution.py:127
  149.3 16.6 %collective-permute-start = (bf16[2,64,256]{2,1,0:T(8,128)(2,1)S(1)}, bf16[2,64,256]{2,1,0:T(8,128)(2,1)S(1)}, u32[]{:S(2)}, u32[]{:S(2)}) collective-permute-start(bf16[2,64,256]{2,1,0:T(8,128)(2,1)S(1)} %slice_bitcast_fusion.1), channel_id=1, source_target_pairs={{0,1},{1,2},{2,3},{4,5},{5,6},{6,7},{8,9},{9,10},{10,11},{12,13},{... | collective-permute-start | bytes 196616 | tf_op jit(solution)/shard_map/ppermute | solution.py:13
  157.8 8.1 %copy-start.17 = (bf16[6,64,256]{2,1,0:T(8,128)(2,1)}, bf16[6,64,256]{2,1,0:T(8,128)(2,1)S(1)}, u32[]{:S(2)}) copy-start(bf16[6,64,256]{2,1,0:T(8,128)(2,1)S(1)} %slice_bitcast_fusion) | copy-start | bytes 589828
  250.3 1.2 copy-start.11
  251.9 0.7 copy-start.9
  251.9 23.9 %copy-start.5 = (bf16[8,64,256]{2,1,0:T(8,128)(2,1)}, bf16[8,64,256]{2,1,0:T(8,128)(2,1)S(1)}, u32[]{:S(2)}) copy-start(bf16[8,64,256]{2,1,0:T(8,128)(2,1)S(1)} %get-tuple-element.27) | copy-start | bytes 786436
  251.9 23.9 %copy-start.7 = (bf16[8,64,256]{2,1,0:T(8,128)(2,1)}, bf16[8,64,256]{2,1,0:T(8,128)(2,1)S(1)}, u32[]{:S(2)}) copy-start(bf16[8,64,256]{2,1,0:T(8,128)(2,1)S(1)} %get-tuple-element.28) | copy-start | bytes 786436
  265.1 10.2 %copy-start.22 = (s32[2,8]{1,0:T(2,128)S(1)}, s32[2,8]{1,0:T(2,128)}, u32[]{:S(2)}) copy-start(s32[2,8]{1,0:T(2,128)} %param.17) | copy-start | bytes 196
  267.3 8.2 %copy-start.18 = (bf16[6,64,256]{2,1,0:T(8,128)(2,1)S(1)}, bf16[6,64,256]{2,1,0:T(8,128)(2,1)}, u32[]{:S(2)}) copy-start(bf16[6,64,256]{2,1,0:T(8,128)(2,1)} %copy-done.17) | copy-start | bytes 589828
  267.3 8.5 %copy-start.13 = (bf16[1,8,64,256]{3,2,1,0:T(8,128)(2,1)S(1)}, bf16[1,8,64,256]{3,2,1,0:T(8,128)(2,1)}, u32[]{:S(2)}) copy-start(bf16[1,8,64,256]{3,2,1,0:T(8,128)(2,1)} %param.10) | copy-start | bytes 786436
  267.3 30.0 %all-to-all-start = ((bf16[16,2,16384]{2,1,0:T(2,128)(2,1)}), bf16[16,2,16384]{2,1,0:T(2,128)(2,1)S(1)}, u32[]{:S(2)}, u32[]{:S(2)}) async-start(bf16[16,2,16384]{2,1,0:T(2,128)(2,1)} %reshape.254), calls=%async_computation | async-start | bytes 2097152 | tf_op jit(solution)/shard_map/all_to_all | solution.py:106
  306.5 2.3 copy-start.3
  318.0 13.4 %copy-start.6 = (bf16[8,64,256]{2,1,0:T(8,128)(2,1)S(1)}, bf16[8,64,256]{2,1,0:T(8,128)(2,1)}, u32[]{:S(2)}) copy-start(bf16[8,64,256]{2,1,0:T(8,128)(2,1)} %copy-done.5) | copy-start | bytes 786436
  318.0 13.4 %copy-start.8 = (bf16[8,64,256]{2,1,0:T(8,128)(2,1)S(1)}, bf16[8,64,256]{2,1,0:T(8,128)(2,1)}, u32[]{:S(2)}) copy-start(bf16[8,64,256]{2,1,0:T(8,128)(2,1)} %copy-done.7) | copy-start | bytes 786436
  322.7 8.7 %copy-start.10 = (bf16[8,64,256]{2,1,0:T(8,128)(2,1)S(1)}, bf16[8,64,256]{2,1,0:T(8,128)(2,1)}, u32[]{:S(2)}) copy-start(bf16[8,64,256]{2,1,0:T(8,128)(2,1)} %copy-done.9) | copy-start | bytes 786436
  322.7 11.3 %copy-start.14 = (bf16[1,8,64,256]{3,2,1,0:T(8,128)(2,1)S(1)}, bf16[1,8,64,256]{3,2,1,0:T(8,128)(2,1)}, u32[]{:S(2)}) copy-start(bf16[1,8,64,256]{3,2,1,0:T(8,128)(2,1)} %param.10) | copy-start | bytes 786436
  322.7 11.3 %copy-start.25 = (f32[64]{0:T(128)S(1)}, f32[64]{0:T(128)}, u32[]{:S(2)}) copy-start(f32[64]{0:T(128)} %param.15) | copy-start | bytes 772
  322.7 260.2 %all-to-all-start.1 = ((bf16[16,2,16384]{2,1,0:T(2,128)(2,1)}), bf16[16,2,16384]{2,1,0:T(2,128)(2,1)S(1)}, u32[]{:S(2)}, u32[]{:S(2)}) async-start(bf16[16,2,16384]{2,1,0:T(2,128)(2,1)} %reshape.256), calls=%async_computation.1 | async-start | bytes 2097152 | tf_op jit(solution)/shard_map/all_to_all | solution.py:109
  330.6 246.8 %all-reduce.3.cloned.1.call-start = ((), (), s32[]{:S(2)}) async-start(), calls=%async_computation.4 | async-start | bytes 131072 | tf_op jit(solution)/shard_map/psum | solution.py:177
  335.7 245.5 %copy-start.16 = (f32[8,64,256]{2,1,0:T(8,128)S(1)}, f32[8,64,256]{2,1,0:T(8,128)}, u32[]{:S(2)}) copy-start(f32[8,64,256]{2,1,0:T(8,128)} %fusion.4) | copy-start | bytes 1572868
  336.4 242.5 %collective-permute-start.1 = (bf16[2,128,256]{2,1,0:T(8,128)(2,1)}, bf16[2,128,256]{2,1,0:T(8,128)(2,1)}, u32[]{:S(2)}, u32[]{:S(2)}) collective-permute-start(bf16[2,128,256]{2,1,0:T(8,128)(2,1)} %fusion.50), channel_id=1, source_target_pairs={{1,0},{2,1},{3,2},{5,4},{6,5},{7,6},{9,8},{10,9},{11,10},{13,12},{... | collective-permute-start | bytes 393224 | tf_op jit(solution)/shard_map/ppermute | solution.py:13
  592.1 2.3 copy-start.4
  594.4 1.0 copy-start.15
  594.4 2.7 copy-start.20
Sparse Core Ops, SparseCore 0:
  337.6 239.8 all-reduce.2
where the time goes:
time: 688 us; the launch traced here: 681 us
  waiting for transfers between devices  286 us (42%)
  other arithmetic  183 us (27%)
  blocking collectives  75 us (11%)
  local copies, waits for them, and re-layouts  58.8 us (9%)
  starting transfers between devices  45.2 us (7%)
  matrix products  18.1 us (3%)
  between operations  14.7 us (2%)
    psum x1, waiting for transfers between devices, body(): lax.psum((grad_conv_w, grad_conv_b, grad_mix_w, grad_mix_b), ('dp', 'spac...  237 us
    scatter-add x2, other arithmetic, back_finish(): total.at[:, :, send_rows[0]].add(returned * live_slots.astype(jnp.float32))  143 us
    psum x1, blocking collectives, body(): lax.psum((grad_conv_w, grad_conv_b, grad_mix_w, grad_mix_b), ('dp', 'spac...  75 us
    unnamed x63, local copies, waits for them, and re-layouts  26.4 us
    all_to_all x1, waiting for transfers between devices, body(): lax.all_to_all(packed_one, 'space', split_axis=2, concat_axis=2, tiled=True)  21.2 us
    all_to_all x1, waiting for transfers between devices, body(): lax.all_to_all(back_start(back_two, adj_tiles, tile_cols, send_rows), 'sp...  18.7 us
  transfers between devices with their start and end apart: 7, of which 5 were waited for; matrix products, arithmetic and copies ran while one was open for 3% of the time, Pallas kernels for 0%

commit v1 on v0

--- a/solution.py
+++ b/solution.py
@@ -175,7 +175,7 @@
     )
     grad_conv_b = jnp.sum(backward_preactivation.astype(jnp.float32), axis=(0, 2))
     grad_conv_w, grad_conv_b, grad_mix_w, grad_mix_b = lax.psum(
-        (grad_conv_w, grad_conv_b, grad_mix_w, grad_mix_b), ("dp", "space", "tm")
+        lax.psum((grad_conv_w, grad_conv_b, grad_mix_w, grad_mix_b), ("space", "tm")), "dp"
     )
     cell_count = (
         inputs.shape[0]

time: 688 us -> 910 us (1.32)
  the two profiles are of different devices: /device:TPU:1 before, /device:TPU:32 now
where the time goes in v1:
time: 910 us; the launch traced here: 902 us
  blocking collectives  325 us (36%)
  waiting for transfers between devices  276 us (30%)
  other arithmetic  183 us (20%)
  local copies, waits for them, and re-layouts  58.6 us (6%)
  starting transfers between devices  27.6 us (3%)
  matrix products  17.3 us (2%)
  between operations  14.7 us (2%)
    psum x1, blocking collectives, body(): lax.psum((grad_conv_w, grad_conv_b, grad_mix_w, grad_mix_b), ('space', 't...  308 us
    psum x1, waiting for transfers between devices, body(): lax.psum((grad_conv_w, grad_conv_b, grad_mix_w, grad_mix_b), ('space', 't...  168 us
    scatter-add x2, other arithmetic, back_finish(): total.at[:, :, send_rows[0]].add(returned * live_slots.astype(jnp.float32))  143 us
    psum x1, waiting for transfers between devices, body(): lax.psum(lax.psum((grad_conv_w, grad_conv_b, grad_mix_w, grad_mix_b), ('s...  44.3 us
    unnamed x69, local copies, waits for them, and re-layouts  26.4 us
    all_to_all x1, waiting for transfers between devices, body(): lax.all_to_all(packed_one, 'space', split_axis=2, concat_axis=2, tiled=True)  23.3 us
    all_to_all x1, waiting for transfers between devices, body(): lax.all_to_all(back_start(back_two, adj_tiles, tile_cols, send_rows), 'sp...  22.2 us
    all_to_all x1, waiting for transfers between devices, body(): lax.all_to_all(back_start(back_one, adj_tiles, tile_cols, send_rows), 'sp...  18.7 us
  transfers between devices with their start and end apart: 8, of which 5 were waited for; matrix products, arithmetic and copies ran while one was open for 2% of the time, Pallas kernels for 0%

profile of v1, /device:TPU:32, one launch (start us, length us, event | category | flops | bytes accessed | tf_op | source)
XLA Modules:
  0.0 902.5 jit_solution(10135946634033348608)
XLA Ops:
  9.4 1.4 convolution_bitcast_fusion.2
  10.7 1.5 copy.81
  12.5 3.5 scatter_fusion.1
  17.3 2.2 reshape.258
  19.6 8.7 all-to-all-start.2
  29.1 1.9 scatter_fusion
  31.9 22.2 %all-to-all-done.2 = bf16[16,2,16384]{2,1,0:T(2,128)(2,1)} async-done(((bf16[16,2,16384]{2,1,0:T(2,128)(2,1)}), bf16[16,2,16384]{2,1,0:T(2,128)(2,1)}, u32[]{:S(2)}, u32[]{:S(2)}) %all-to-all-start.2) | async-done | bytes 1048608 | tf_op jit(solution)/shard_map/all_to_all | solution.py:116
  54.1 3.8 reshape.259
  57.8 3.1 convert_multiply_fusion.1
  61.0 71.3 %scatter_fusion.2 = f32[8,64,256]{1,0,2:T(8,128)S(1)} fusion(f32[8,64,256]{1,0,2:T(8,128)S(1)} %copy.84, s32[1024]{0:T(1024)S(1)} %reshape.131, f32[1024,8,64]{2,1,0:T(8,128)} %bitcast.273), kind=kCustom, calls=%fused_computation.6 | custom fusion | flops 524288 | bytes 6295552 | tf_op jit(solution)/shard_map/scatter-add | solution.py:73
  133.7 1.5 copy.89
  135.4 3.5 scatter_fusion.4
  140.1 2.1 copy.124
  142.2 2.2 reshape.260
  144.5 5.3 all-to-all-start.3
  149.8 1.5 collective-permute-start
  152.0 1.3 fusion.1
  154.0 1.9 scatter_fusion.3
  156.6 18.7 %all-to-all-done.3 = bf16[16,2,16384]{2,1,0:T(2,128)(2,1)} async-done(((bf16[16,2,16384]{2,1,0:T(2,128)(2,1)}), bf16[16,2,16384]{2,1,0:T(2,128)(2,1)}, u32[]{:S(2)}, u32[]{:S(2)}) %all-to-all-start.3) | async-done | bytes 1048608 | tf_op jit(solution)/shard_map/all_to_all | solution.py:127
  175.3 3.8 reshape.261
  179.1 3.1 convert_multiply_fusion
  182.2 71.3 %scatter_fusion.5 = f32[8,64,256]{1,0,2:T(8,128)S(1)} fusion(f32[8,64,256]{1,0,2:T(8,128)S(1)} %copy.92, s32[1024]{0:T(1024)S(1)} %reshape.131, f32[1024,8,64]{2,1,0:T(8,128)} %bitcast.272), kind=kCustom, calls=%fused_computation.9 | custom fusion | flops 524288 | bytes 6295552 | tf_op jit(solution)/shard_map/scatter-add | solution.py:73
  255.7 7.6 gather_fusion
  263.3 4.9 fusion.76
  268.2 2.2 reshape.254
  270.5 5.2 all-to-all-start
  277.2 23.3 %all-to-all-done = bf16[16,2,16384]{2,1,0:T(2,128)(2,1)S(1)} async-done(((bf16[16,2,16384]{2,1,0:T(2,128)(2,1)}), bf16[16,2,16384]{2,1,0:T(2,128)(2,1)S(1)}, u32[]{:S(2)}, u32[]{:S(2)}) %all-to-all-start) | async-done | bytes 1048608 | tf_op jit(solution)/shard_map/all_to_all | solution.py:106
  300.5 2.3 reshape.255
  302.8 3.4 pad_maximum_fusion
  306.2 3.3 copy.65
  309.5 2.3 gather_fusion.1
  312.9 3.3 gather_fusion.2
  316.2 4.8 fusion.77
  321.0 4.7 reshape.256
  325.7 5.3 all-to-all-start.1
  334.6 167.7 %all-reduce.5.cloned.1.call-done = f32[2,128,64]{1,2,0:T(8,128)} async-done(((f32[2,128,64]{1,2,0:T(8,128)}), f32[2,128,64]{1,2,0:T(8,128)}) %all-reduce.5.cloned.1.call-update) | async-done | bytes 65552 | tf_op jit(solution)/shard_map/psum | solution.py:178
  503.0 1.6 collective-permute-start.1
  504.8 44.3 %all-reduce.7.cloned.1.call-done = f32[2,128,64]{1,2,0:T(8,128)} async-done(((f32[2,128,64]{1,2,0:T(8,128)}), f32[2,128,64]{1,2,0:T(8,128)}) %all-reduce.7.cloned.1.call-update) | async-done | bytes 65552 | tf_op jit(solution)/shard_map/psum | solution.py:177
  549.1 1.5 broadcast_multiply_fusion.1
  550.6 2.1 fusion.13
  552.9 1.8 fusion.3
  554.6 2.3 reshape.257
  557.0 3.4 pad_maximum_fusion.1
  560.4 3.3 copy.71
  563.7 2.3 gather_fusion.3
  567.0 1.6 fusion.14
  568.7 308.0 %all-reduce = (f32[128]{0:T(128)S(1)}, f32[3,64,64]{1,2,0:T(8,128)S(1)}, f32[64]{0:T(128)S(1)}) all-reduce(f32[128]{0:T(128)S(1)} %convert_reduce_fusion, f32[3,64,64]{1,2,0:T(8,128)S(1)} %pad_maximum_fusion.6, f32[64]{0:T(128)S(1)} %convert_reduce_fusion.1), channel_id=1, replica_groups=mesh['dp'=4,'space'=16,'tm'=4] {'space','tm'}, use_global_device_ids=true, to_apply=%region_9.0 | all-reduce | flops 12480 | bytes 99840 | tf_op jit(solution)/shard_map/psum | solution.py:178
  876.7 17.1 %all-reduce.1 = (f32[128]{0:T(128)S(1)}, f32[3,64,64]{1,2,0:T(8,128)S(1)}, f32[64]{0:T(128)S(1)}) all-reduce(f32[128]{0:T(128)S(1)} %get-tuple-element.24, f32[3,64,64]{1,2,0:T(8,128)S(1)} %get-tuple-element.25, f32[64]{0:T(128)S(1)} %get-tuple-element.26), channel_id=1, replica_groups=mesh['dp'=4,'space'=16,'tm'=4] {'dp'}, use_global_device_ids=true, to_apply=%region_10.0 | all-reduce | flops 12480 | bytes 99840 | tf_op jit(solution)/shard_map/psum | solution.py:177
  (129 shorter events, 22.5 us)
Async XLA Ops:
  17.3 11.0 %copy-start.1 = (bf16[2,8,128,128]{3,2,1,0:T(8,128)(2,1)S(1)}, bf16[2,8,128,128]{3,2,1,0:T(8,128)(2,1)}, u32[]{:S(2)}) copy-start(bf16[2,8,128,128]{3,2,1,0:T(8,128)(2,1)} %param.16) | copy-start | bytes 1572868
  19.6 34.5 %all-to-all-start.2 = ((bf16[16,2,16384]{2,1,0:T(2,128)(2,1)}), bf16[16,2,16384]{2,1,0:T(2,128)(2,1)}, u32[]{:S(2)}, u32[]{:S(2)}) async-start(bf16[16,2,16384]{2,1,0:T(2,128)(2,1)} %reshape.258), calls=%async_computation.2 | async-start | bytes 2097152 | tf_op jit(solution)/shard_map/all_to_all | solution.py:116
  29.0 1.9 copy-start
  29.1 1.9 copy-start.19
  31.0 0.7 copy-start.26
  31.0 0.8 copy-start.27
  132.2 1.0 copy-start.2
  142.2 7.5 copy-start.12
  144.5 7.1 copy-start.21
  144.5 7.5 copy-start.29
  144.5 30.8 %all-to-all-start.3 = ((bf16[16,2,16384]{2,1,0:T(2,128)(2,1)}), bf16[16,2,16384]{2,1,0:T(2,128)(2,1)}, u32[]{:S(2)}, u32[]{:S(2)}) async-start(bf16[16,2,16384]{2,1,0:T(2,128)(2,1)} %reshape.260), calls=%async_computation.3 | async-start | bytes 2097152 | tf_op jit(solution)/shard_map/all_to_all | solution.py:127
  149.8 2.2 collective-permute-start
  151.6 1.7 copy-start.17
  152.0 1.3 copy-start.22
  253.5 1.2 copy-start.11
  255.0 0.7 copy-start.9
  255.0 21.2 %copy-start.5 = (bf16[8,64,256]{2,1,0:T(8,128)(2,1)}, bf16[8,64,256]{2,1,0:T(8,128)(2,1)S(1)}, u32[]{:S(2)}) copy-start(bf16[8,64,256]{2,1,0:T(8,128)(2,1)S(1)} %get-tuple-element.30) | copy-start | bytes 786436
  255.0 21.2 %copy-start.7 = (bf16[8,64,256]{2,1,0:T(8,128)(2,1)}, bf16[8,64,256]{2,1,0:T(8,128)(2,1)S(1)}, u32[]{:S(2)}) copy-start(bf16[8,64,256]{2,1,0:T(8,128)(2,1)S(1)} %get-tuple-element.31) | copy-start | bytes 786436
  268.2 7.5 copy-start.25
  270.5 5.5 copy-start.18
  270.5 5.5 copy-start.23
  270.5 5.8 copy-start.13
  270.5 30.0 %all-to-all-start = ((bf16[16,2,16384]{2,1,0:T(2,128)(2,1)}), bf16[16,2,16384]{2,1,0:T(2,128)(2,1)S(1)}, u32[]{:S(2)}, u32[]{:S(2)}) async-start(bf16[16,2,16384]{2,1,0:T(2,128)(2,1)} %reshape.254), calls=%async_computation | async-start | bytes 2097152 | tf_op jit(solution)/shard_map/all_to_all | solution.py:106
  309.5 2.3 copy-start.3
  321.0 10.0 %copy-start.24 = (f32[1,128,64]{1,2,0:T(8,128)S(1)}, f32[1,128,64]{1,2,0:T(8,128)}, u32[]{:S(2)}) copy-start(f32[1,128,64]{1,2,0:T(8,128)} %convolution_bitcast_fusion.13) | copy-start | bytes 98308
  321.0 10.7 %copy-start.10 = (bf16[8,64,256]{2,1,0:T(8,128)(2,1)S(1)}, bf16[8,64,256]{2,1,0:T(8,128)(2,1)}, u32[]{:S(2)}) copy-start(bf16[8,64,256]{2,1,0:T(8,128)(2,1)} %copy-done.9) | copy-start | bytes 786436
  325.7 6.9 copy-start.6
  325.7 6.9 copy-start.8
  325.7 7.9 copy-start.14
  325.7 7.9 copy-start.28
  325.7 228.9 %all-to-all-start.1 = ((bf16[16,2,16384]{2,1,0:T(2,128)(2,1)}), bf16[16,2,16384]{2,1,0:T(2,128)(2,1)S(1)}, u32[]{:S(2)}, u32[]{:S(2)}) async-start(bf16[16,2,16384]{2,1,0:T(2,128)(2,1)} %reshape.256), calls=%async_computation.1 | async-start | bytes 2097152 | tf_op jit(solution)/shard_map/all_to_all | solution.py:109
  331.0 171.4 %all-reduce.5.cloned.1.call-start = ((), (), s32[]{:S(2)}) async-start(), calls=%async_computation.4 | async-start | bytes 131072 | tf_op jit(solution)/shard_map/psum | solution.py:178
  331.7 217.4 %all-reduce.7.cloned.1.call-start = ((), (), s32[]{:S(2)}) async-start(), calls=%async_computation.5 | async-start | bytes 131072 | tf_op jit(solution)/shard_map/psum | solution.py:177
  334.6 218.3 %copy-start.16 = (f32[8,64,256]{2,1,0:T(8,128)S(1)}, f32[8,64,256]{2,1,0:T(8,128)}, u32[]{:S(2)}) copy-start(f32[8,64,256]{2,1,0:T(8,128)} %fusion.4) | copy-start | bytes 1572868
  503.0 47.6 %collective-permute-start.1 = (bf16[2,128,256]{2,1,0:T(8,128)(2,1)}, bf16[2,128,256]{2,1,0:T(8,128)(2,1)}, u32[]{:S(2)}, u32[]{:S(2)}) collective-permute-start(bf16[2,128,256]{2,1,0:T(8,128)(2,1)} %fusion.50), channel_id=1, source_target_pairs={{1,0},{2,1},{3,2},{5,4},{6,5},{7,6},{9,8},{10,9},{11,10},{13,12},{... | collective-permute-start | bytes 393224 | tf_op jit(solution)/shard_map/ppermute | solution.py:13
  563.7 2.3 copy-start.4
  566.0 1.0 copy-start.15
  566.0 2.7 copy-start.20
Sparse Core Ops, SparseCore 0:
  335.8 166.4 all-reduce.4
  504.6 44.4 all-reduce.6
